TPU v7x, 32 devices: a whole 2x2x4 slice. The times are simulated.
32 devices in a mesh: grp: 2 (over x), had: 16 (over z, y, core).
Axes of the slice: x: 2, y: 2, z: 4, core: 2. Of those that a mesh axis runs over, the one named last changes fastest.
Arguments:
- source_slabs: bfloat16 [512, 128, 128], P(('grp', 'had')), parts along dimension 0, may hold values from -6 to 6
- sink_slabs: bfloat16 [512, 128, 128], P(('grp', 'had')), parts along dimension 0, may hold values from -6 to 6
- perambulators: bfloat16 [4, 2, 128, 128], P('grp'), parts along dimension 0, may hold values from -0.5 to 0.5
- send_pick: int32 [32, 16], P(('grp', 'had')), parts along dimension 0, may hold values from 0 to 15
- graph_slot: int32 [32, 512, 2], P(('grp', 'had')), parts along dimension 0, may hold values from 0 to 15
- graph_sink: int32 [32, 512, 2], P(('grp', 'had')), parts along dimension 0, may hold values from 0 to 15
- graph_count: int32 [32], P(('grp', 'had')), parts along dimension 0, may hold values from 64 to 512, as said below
- pair_list: int32 [256, 2], P(('grp', 'had')), parts along dimension 0, may hold values from 0 to 15
Outputs:
- edge_matrices: bfloat16 [32, 128, 128], P(('grp', 'had')), parts along dimension 0
- pair_products: bfloat16 [256, 128, 128], P(('grp', 'had')), parts along dimension 0
There are 2 independent parts, one for each index of `grp`. A program takes and returns all parts, laid end to end along the dimension named above; each array names one. Nothing has to cross between parts.
Inputs may be any that keep to these rules, and one draw needn't show every extreme that they name: Some reader uses all 512 graph slots; slots from graph_count on are unused.
All inputs are finite; a program needn't handle non-finite values.
Results may differ from a plain program's by a relative error of at most 0.012.
Values may be sent and summed in bfloat16 or wider, within the bound.
A program may use at most 64 MiB of HBM per device.

v0:
```python
import math
import jax
import jax.numpy as jnp
from jax import lax
from jax.sharding import PartitionSpec as P


def shards(
    source_slabs,
    sink_slabs,
    perambulators,
    send_pick,
    graph_slot,
    graph_sink,
    graph_count,
    pair_list,
):
    my_index = lax.axis_index("had")
    evecs = source_slabs.shape[1]
    per_device = source_slabs.shape[0]
    root_scale = 1.0 / math.sqrt(evecs)
    edge_scale = 1.0 / math.sqrt(evecs * graph_slot.shape[1])
    timeslice = my_index * per_device // evecs
    local_peram = lax.dynamic_index_in_dim(perambulators, timeslice, 0, keepdims=False)
    first_turn = jnp.einsum(
        "xa,jab->xjb", local_peram[0], source_slabs, preferred_element_type=jnp.float32
    ).astype(jnp.bfloat16)
    pick_row = send_pick[0]
    second_turn = jnp.einsum(
        "xjb,yb->xjy", first_turn, local_peram[1], preferred_element_type=jnp.float32
    ).astype(jnp.bfloat16)
    outgoing = jnp.take(second_turn, pick_row, axis=1)
    received = lax.all_to_all(outgoing, "had", split_axis=1, concat_axis=1, tiled=True)
    graph_rows = graph_slot.shape[1]
    block_width = min(64, graph_rows)
    slot_table = graph_slot[0]
    sink_table = graph_sink[0]
    graph_total = graph_count[0]

    def factor(slots, sinks):
        gathered = jnp.take(received, slots, axis=1)
        resident = jnp.take(sink_slabs, sinks, axis=0)
        product = jnp.einsum("gxb,agb->gxa", resident, gathered, preferred_element_type=jnp.float32)
        return (product * root_scale).astype(jnp.bfloat16)

    def accumulate(block_index, running_sum):
        offset = block_index * block_width
        slots = lax.dynamic_slice_in_dim(slot_table, offset, block_width, 0)
        sinks = lax.dynamic_slice_in_dim(sink_table, offset, block_width, 0)
        is_valid = (offset + jnp.arange(block_width, dtype=jnp.int32) < graph_total).astype(
            jnp.bfloat16
        )
        left_side = factor(slots[:, 0], sinks[:, 0]) * is_valid[:, None, None]
        right_side = factor(slots[:, 1], sinks[:, 1])
        return running_sum + jnp.einsum(
            "gxa,gay->xy", left_side, right_side, preferred_element_type=jnp.float32
        )

    block_count = (graph_total + block_width - 1) // block_width
    summed = lax.fori_loop(0, block_count, accumulate, jnp.zeros((evecs, evecs), jnp.float32))
    edge_local = (summed * edge_scale).astype(jnp.bfloat16)[None]
    left_ids = pair_list[:, 0]
    right_ids = pair_list[:, 1]
    shard_rows = lax.all_gather(edge_local, "had", axis=0, tiled=True)
    row_ids = jnp.arange(shard_rows.shape[0], dtype=jnp.int32)
    left_select = (left_ids[:, None] == row_ids[None, :]).astype(jnp.bfloat16)
    right_select = (right_ids[:, None] == row_ids[None, :]).astype(jnp.bfloat16)
    left_part = jnp.einsum(
        "pn,nxy->pxy", left_select, shard_rows, preferred_element_type=jnp.float32
    )
    right_part = jnp.einsum(
        "pn,nxy->pxy", right_select, shard_rows, preferred_element_type=jnp.float32
    )
    left_edges = left_part.astype(jnp.bfloat16)
    right_edges = right_part.astype(jnp.bfloat16)
    product = jnp.einsum(
        "pxa,pay->pxy", left_edges, right_edges, preferred_element_type=jnp.float32
    )
    pair_products = (product * root_scale).astype(jnp.bfloat16)
    return (edge_local, pair_products)


def solution(mesh):
    return jax.shard_map(
        shards,
        mesh=mesh,
        in_specs=(
            P(("grp", "had"), None, None),
            P(("grp", "had"), None, None),
            P("grp", None, None, None),
            P(("grp", "had"), None),
            P(("grp", "had"), None, None),
            P(("grp", "had"), None, None),
            P(("grp", "had")),
            P(("grp", "had"), None),
        ),
        out_specs=(P(("grp", "had"), None, None), P(("grp", "had"), None, None)),
        check_vma=False,
    )
```

profile of v0, /device:TPU:0, one launch (start us, length us, event | category | flops | bytes accessed | tf_op | source)
XLA Modules:
  0.0 210.6 jit_solution(10187311681063074676)
XLA Ops:
  0.6 0.0 copy-start
  0.7 0.7 fusion.45
  1.4 0.7 compare_and_fusion.4
  2.0 0.0 copy-done
  2.1 0.0 copy-start.2
  2.1 0.0 copy-start.1
  2.1 1.3 convolution_convert_fusion
  3.4 0.6 gather_fusion.4
  4.1 0.9 select_bitcast_fusion
  5.0 7.4 %all-to-all-start = ((bf16[128,16,128]{2,0,1:T(8,128)(2,1)}), bf16[128,16,128]{2,0,1:T(8,128)(2,1)S(1)}, u32[]{:S(2)}, u32[]{:S(2)}) async-start(bf16[128,16,128]{2,0,1:T(8,128)(2,1)} %select_bitcast_fusion), calls=%async_computation | async-start | bytes 1048576 | tf_op jit(solution)/shard_map/all_to_all | solution.py:33
  13.1 0.0 copy-done.2
  13.1 13.6 %all-to-all-done = bf16[128,16,128]{2,0,1:T(8,128)(2,1)S(1)} async-done(((bf16[128,16,128]{2,0,1:T(8,128)(2,1)}), bf16[128,16,128]{2,0,1:T(8,128)(2,1)S(1)}, u32[]{:S(2)}, u32[]{:S(2)}) %all-to-all-start) | async-done | bytes 524320 | tf_op jit(solution)/shard_map/all_to_all | solution.py:33
  26.7 0.0 copy-done.1
  26.7 81.4 %while.10 = (s32[]{:T(128)}, f32[128,128]{1,0:T(8,128)S(1)}, s32[]{:T(128)}, s32[512,2]{0,1:T(2,128)}, bf16[16,128,128]{2,1,0:T(8,128)(2,1)S(1)}, /*index=5*/s32...) while((s32[]{:T(128)}, f32[128,128]{1,0:T(8,128)S(1)}, ...), condition=%wide.region_1.4_spmd, body=%wide.region_0.3_spmd.sunk | while | flops 814765760 | bytes 29514672 | solution.py:60
  26.7 0.8 constant_dynamic-slice_fusion.3
  27.5 2.1 %gather_fusion = bf16[64,128,128]{2,1,0:T(8,128)(2,1)} fusion(bf16[128,16,128]{2,0,1:T(8,128)(2,1)S(1)} %get-tuple-element.188, s32[1024]{0:T(1024)S(1)} %pad_clamp_fusion.9), kind=kCustom, calls=%fused_computation.3.clone.clone.1 | custom fusion | bytes 4194560 | tf_op jit(solution)/shard_map/while/body/jit(_take)/gather | solution.py:41
  29.7 2.1 %gather_fusion.1 = bf16[64,128,128]{2,1,0:T(8,128)(2,1)} fusion(bf16[16,128,128]{2,1,0:T(8,128)(2,1)S(1)} %get-tuple-element.186, s32[1024]{0:T(1024)S(1)} %pad_clamp_fusion.10), kind=kCustom, calls=%fused_computation.2.clone.clone.1 | custom fusion | bytes 4194560 | tf_op jit(solution)/shard_map/while/body/jit(_take)/gather | solution.py:42
  31.8 5.2 %multiply_convert_fusion.4 = bf16[64,128,128]{2,1,0:T(8,128)(2,1)} fusion(bf16[64,128,128]{2,1,0:T(8,128)(2,1)} %gather_fusion, bf16[64,128,128]{2,1,0:T(8,128)(2,1)} %gather_fusion.1, pred[64]{0:T(512)(128)(4,1)S(1)} %get-tuple-element.152, pred[64]{0:T(512)(128)(4,1)S(1)} %get-tuple-element.153), kind=kOutput, calls=%fused_computation.5.clone.1 | convolution fusion | flops 272629760 | bytes 6291584 | tf_op jit(solution)/shard_map/while/body/gxb,agb->gxa/dot_general | solution.py:43
  37.0 2.1 %gather_fusion.2 = bf16[64,128,128]{2,1,0:T(8,128)(2,1)} fusion(bf16[128,16,128]{2,0,1:T(8,128)(2,1)S(1)} %get-tuple-element.188, s32[1024]{0:T(1024)S(1)} %pad_clamp_fusion.11), kind=kCustom, calls=%fused_computation.1.clone.clone.1 | custom fusion | bytes 4194560 | tf_op jit(solution)/shard_map/while/body/jit(_take)/gather | solution.py:41
  39.1 2.1 %gather_fusion.3 = bf16[64,128,128]{2,1,0:T(8,128)(2,1)} fusion(bf16[16,128,128]{2,1,0:T(8,128)(2,1)S(1)} %get-tuple-element.186, s32[1024]{0:T(1024)S(1)} %pad_clamp_fusion.12), kind=kCustom, calls=%fused_computation.clone.clone.1 | custom fusion | bytes 4194560 | tf_op jit(solution)/shard_map/while/body/jit(_take)/gather | solution.py:42
  41.3 0.6 compare_convert_fusion.2
  41.9 5.1 %fusion.64 = f32[128,128]{1,0:T(8,128)S(1)} fusion(f32[128,128]{1,0:T(8,128)S(1)} %get-tuple-element.171, bf16[64,128,128]{2,1,0:T(8,128)(2,1)} %multiply_convert_fusion.4, bf16[64,128,128]{2,1,0:T(8,128)(2,1)} %gather_fusion.2, bf16[64,128,128]{2,1,0:T(8,128)(2,1)} %gather_fusion.3, pred[64]{0:T(512)(128)(4,1)S(1)} %get-tuple-element.156, ...), kind=kOutput, calls=%fused_computation.20.clone.1 | convolution fusion | flops 542130176 | bytes 6422784 | tf_op jit(solution)/shard_map/while/body/gxa,gay->xy/dot_general | solution.py:55
  47.1 0.8 constant_dynamic-slice_fusion.3
  47.9 2.1 %gather_fusion = bf16[64,128,128]{2,1,0:T(8,128)(2,1)} fusion(bf16[128,16,128]{2,0,1:T(8,128)(2,1)S(1)} %get-tuple-element.188, s32[1024]{0:T(1024)S(1)} %pad_clamp_fusion.9), kind=kCustom, calls=%fused_computation.3.clone.clone.1 | custom fusion | bytes 4194560 | tf_op jit(solution)/shard_map/while/body/jit(_take)/gather | solution.py:41
  50.0 2.1 %gather_fusion.1 = bf16[64,128,128]{2,1,0:T(8,128)(2,1)} fusion(bf16[16,128,128]{2,1,0:T(8,128)(2,1)S(1)} %get-tuple-element.186, s32[1024]{0:T(1024)S(1)} %pad_clamp_fusion.10), kind=kCustom, calls=%fused_computation.2.clone.clone.1 | custom fusion | bytes 4194560 | tf_op jit(solution)/shard_map/while/body/jit(_take)/gather | solution.py:42
  52.1 5.2 %multiply_convert_fusion.4 = bf16[64,128,128]{2,1,0:T(8,128)(2,1)} fusion(bf16[64,128,128]{2,1,0:T(8,128)(2,1)} %gather_fusion, bf16[64,128,128]{2,1,0:T(8,128)(2,1)} %gather_fusion.1, pred[64]{0:T(512)(128)(4,1)S(1)} %get-tuple-element.152, pred[64]{0:T(512)(128)(4,1)S(1)} %get-tuple-element.153), kind=kOutput, calls=%fused_computation.5.clone.1 | convolution fusion | flops 272629760 | bytes 6291584 | tf_op jit(solution)/shard_map/while/body/gxb,agb->gxa/dot_general | solution.py:43
  57.4 2.1 %gather_fusion.2 = bf16[64,128,128]{2,1,0:T(8,128)(2,1)} fusion(bf16[128,16,128]{2,0,1:T(8,128)(2,1)S(1)} %get-tuple-element.188, s32[1024]{0:T(1024)S(1)} %pad_clamp_fusion.11), kind=kCustom, calls=%fused_computation.1.clone.clone.1 | custom fusion | bytes 4194560 | tf_op jit(solution)/shard_map/while/body/jit(_take)/gather | solution.py:41
  59.5 2.1 %gather_fusion.3 = bf16[64,128,128]{2,1,0:T(8,128)(2,1)} fusion(bf16[16,128,128]{2,1,0:T(8,128)(2,1)S(1)} %get-tuple-element.186, s32[1024]{0:T(1024)S(1)} %pad_clamp_fusion.12), kind=kCustom, calls=%fused_computation.clone.clone.1 | custom fusion | bytes 4194560 | tf_op jit(solution)/shard_map/while/body/jit(_take)/gather | solution.py:42
  61.6 0.6 compare_convert_fusion.2
  62.3 5.1 %fusion.64 = f32[128,128]{1,0:T(8,128)S(1)} fusion(f32[128,128]{1,0:T(8,128)S(1)} %get-tuple-element.171, bf16[64,128,128]{2,1,0:T(8,128)(2,1)} %multiply_convert_fusion.4, bf16[64,128,128]{2,1,0:T(8,128)(2,1)} %gather_fusion.2, bf16[64,128,128]{2,1,0:T(8,128)(2,1)} %gather_fusion.3, pred[64]{0:T(512)(128)(4,1)S(1)} %get-tuple-element.156, ...), kind=kOutput, calls=%fused_computation.20.clone.1 | convolution fusion | flops 542130176 | bytes 6422784 | tf_op jit(solution)/shard_map/while/body/gxa,gay->xy/dot_general | solution.py:55
  67.4 0.8 constant_dynamic-slice_fusion.3
  68.2 2.1 %gather_fusion = bf16[64,128,128]{2,1,0:T(8,128)(2,1)} fusion(bf16[128,16,128]{2,0,1:T(8,128)(2,1)S(1)} %get-tuple-element.188, s32[1024]{0:T(1024)S(1)} %pad_clamp_fusion.9), kind=kCustom, calls=%fused_computation.3.clone.clone.1 | custom fusion | bytes 4194560 | tf_op jit(solution)/shard_map/while/body/jit(_take)/gather | solution.py:41
  70.4 2.1 %gather_fusion.1 = bf16[64,128,128]{2,1,0:T(8,128)(2,1)} fusion(bf16[16,128,128]{2,1,0:T(8,128)(2,1)S(1)} %get-tuple-element.186, s32[1024]{0:T(1024)S(1)} %pad_clamp_fusion.10), kind=kCustom, calls=%fused_computation.2.clone.clone.1 | custom fusion | bytes 4194560 | tf_op jit(solution)/shard_map/while/body/jit(_take)/gather | solution.py:42
  72.5 5.2 %multiply_convert_fusion.4 = bf16[64,128,128]{2,1,0:T(8,128)(2,1)} fusion(bf16[64,128,128]{2,1,0:T(8,128)(2,1)} %gather_fusion, bf16[64,128,128]{2,1,0:T(8,128)(2,1)} %gather_fusion.1, pred[64]{0:T(512)(128)(4,1)S(1)} %get-tuple-element.152, pred[64]{0:T(512)(128)(4,1)S(1)} %get-tuple-element.153), kind=kOutput, calls=%fused_computation.5.clone.1 | convolution fusion | flops 272629760 | bytes 6291584 | tf_op jit(solution)/shard_map/while/body/gxb,agb->gxa/dot_general | solution.py:43
  77.7 2.1 %gather_fusion.2 = bf16[64,128,128]{2,1,0:T(8,128)(2,1)} fusion(bf16[128,16,128]{2,0,1:T(8,128)(2,1)S(1)} %get-tuple-element.188, s32[1024]{0:T(1024)S(1)} %pad_clamp_fusion.11), kind=kCustom, calls=%fused_computation.1.clone.clone.1 | custom fusion | bytes 4194560 | tf_op jit(solution)/shard_map/while/body/jit(_take)/gather | solution.py:41
  79.8 2.1 %gather_fusion.3 = bf16[64,128,128]{2,1,0:T(8,128)(2,1)} fusion(bf16[16,128,128]{2,1,0:T(8,128)(2,1)S(1)} %get-tuple-element.186, s32[1024]{0:T(1024)S(1)} %pad_clamp_fusion.12), kind=kCustom, calls=%fused_computation.clone.clone.1 | custom fusion | bytes 4194560 | tf_op jit(solution)/shard_map/while/body/jit(_take)/gather | solution.py:42
  82.0 0.6 compare_convert_fusion.2
  82.6 5.1 %fusion.64 = f32[128,128]{1,0:T(8,128)S(1)} fusion(f32[128,128]{1,0:T(8,128)S(1)} %get-tuple-element.171, bf16[64,128,128]{2,1,0:T(8,128)(2,1)} %multiply_convert_fusion.4, bf16[64,128,128]{2,1,0:T(8,128)(2,1)} %gather_fusion.2, bf16[64,128,128]{2,1,0:T(8,128)(2,1)} %gather_fusion.3, pred[64]{0:T(512)(128)(4,1)S(1)} %get-tuple-element.156, ...), kind=kOutput, calls=%fused_computation.20.clone.1 | convolution fusion | flops 542130176 | bytes 6422784 | tf_op jit(solution)/shard_map/while/body/gxa,gay->xy/dot_general | solution.py:55
  87.8 0.8 constant_dynamic-slice_fusion.3
  88.6 2.1 %gather_fusion = bf16[64,128,128]{2,1,0:T(8,128)(2,1)} fusion(bf16[128,16,128]{2,0,1:T(8,128)(2,1)S(1)} %get-tuple-element.188, s32[1024]{0:T(1024)S(1)} %pad_clamp_fusion.9), kind=kCustom, calls=%fused_computation.3.clone.clone.1 | custom fusion | bytes 4194560 | tf_op jit(solution)/shard_map/while/body/jit(_take)/gather | solution.py:41
  90.7 2.1 %gather_fusion.1 = bf16[64,128,128]{2,1,0:T(8,128)(2,1)} fusion(bf16[16,128,128]{2,1,0:T(8,128)(2,1)S(1)} %get-tuple-element.186, s32[1024]{0:T(1024)S(1)} %pad_clamp_fusion.10), kind=kCustom, calls=%fused_computation.2.clone.clone.1 | custom fusion | bytes 4194560 | tf_op jit(solution)/shard_map/while/body/jit(_take)/gather | solution.py:42
  92.8 5.2 %multiply_convert_fusion.4 = bf16[64,128,128]{2,1,0:T(8,128)(2,1)} fusion(bf16[64,128,128]{2,1,0:T(8,128)(2,1)} %gather_fusion, bf16[64,128,128]{2,1,0:T(8,128)(2,1)} %gather_fusion.1, pred[64]{0:T(512)(128)(4,1)S(1)} %get-tuple-element.152, pred[64]{0:T(512)(128)(4,1)S(1)} %get-tuple-element.153), kind=kOutput, calls=%fused_computation.5.clone.1 | convolution fusion | flops 272629760 | bytes 6291584 | tf_op jit(solution)/shard_map/while/body/gxb,agb->gxa/dot_general | solution.py:43
  98.1 2.1 %gather_fusion.2 = bf16[64,128,128]{2,1,0:T(8,128)(2,1)} fusion(bf16[128,16,128]{2,0,1:T(8,128)(2,1)S(1)} %get-tuple-element.188, s32[1024]{0:T(1024)S(1)} %pad_clamp_fusion.11), kind=kCustom, calls=%fused_computation.1.clone.clone.1 | custom fusion | bytes 4194560 | tf_op jit(solution)/shard_map/while/body/jit(_take)/gather | solution.py:41
  100.2 2.1 %gather_fusion.3 = bf16[64,128,128]{2,1,0:T(8,128)(2,1)} fusion(bf16[16,128,128]{2,1,0:T(8,128)(2,1)S(1)} %get-tuple-element.186, s32[1024]{0:T(1024)S(1)} %pad_clamp_fusion.12), kind=kCustom, calls=%fused_computation.clone.clone.1 | custom fusion | bytes 4194560 | tf_op jit(solution)/shard_map/while/body/jit(_take)/gather | solution.py:42
  102.3 0.6 compare_convert_fusion.2
  103.0 5.1 %fusion.64 = f32[128,128]{1,0:T(8,128)S(1)} fusion(f32[128,128]{1,0:T(8,128)S(1)} %get-tuple-element.171, bf16[64,128,128]{2,1,0:T(8,128)(2,1)} %multiply_convert_fusion.4, bf16[64,128,128]{2,1,0:T(8,128)(2,1)} %gather_fusion.2, bf16[64,128,128]{2,1,0:T(8,128)(2,1)} %gather_fusion.3, pred[64]{0:T(512)(128)(4,1)S(1)} %get-tuple-element.156, ...), kind=kOutput, calls=%fused_computation.20.clone.1 | convolution fusion | flops 542130176 | bytes 6422784 | tf_op jit(solution)/shard_map/while/body/gxa,gay->xy/dot_general | solution.py:55
  108.1 0.6 fusion.50
  108.7 100.1 %all-gather = bf16[2048,128]{1,0:T(8,128)(2,1)S(1)} all-gather(bf16[128,128]{1,0:T(8,128)(2,1)S(1)} %multiply_convert_fusion.2), channel_id=2, replica_groups=mesh['grp'=2,'had'=16] {'had'}, dimensions={0}, use_global_device_ids=true | all-gather | bytes 557056 | tf_op jit(solution)/shard_map/all_gather | solution.py:64
  208.8 0.4 fusion.35
  209.2 0.4 fusion.37
  209.6 0.9 fusion.34
  (28 shorter events, 0.2 us)
Async XLA Ops:
  0.6 1.4 copy-start
  2.1 11.0 %copy-start.2 = (s32[8,2]{0,1:T(2,128)S(1)}, s32[8,2]{0,1:T(2,128)}, u32[]{:S(2)}) copy-start(s32[8,2]{0,1:T(2,128)} %param.21) | copy-start | bytes 196
  2.1 24.6 %copy-start.1 = (bf16[16,128,128]{2,1,0:T(8,128)(2,1)S(1)}, bf16[16,128,128]{2,1,0:T(8,128)(2,1)}, u32[]{:S(2)}) copy-start(bf16[16,128,128]{2,1,0:T(8,128)(2,1)} %param.15) | copy-start | bytes 1572868
  5.0 21.7 %all-to-all-start = ((bf16[128,16,128]{2,0,1:T(8,128)(2,1)}), bf16[128,16,128]{2,0,1:T(8,128)(2,1)S(1)}, u32[]{:S(2)}, u32[]{:S(2)}) async-start(bf16[128,16,128]{2,0,1:T(8,128)(2,1)} %select_bitcast_fusion), calls=%async_computation | async-start | bytes 1048576 | tf_op jit(solution)/shard_map/all_to_all | solution.py:33
where the time goes:
time: 211 us
  blocking collectives  100 us (47%)
  matrix products  44.2 us (21%)
  local copies, waits for them, and re-layouts  37.9 us (18%)
  waiting for transfers between devices  13.6 us (6%)
  starting transfers between devices  7.41 us (4%)
  other arithmetic  5.68 us (3%)
    all_gather x1, blocking collectives, shards(): shard_rows = lax.all_gather(edge_local, 'had', axis=0, tiled=True)  100 us
    dot_general x4, matrix products, factor(): jnp.einsum('gxb,agb->gxa', resident, gathered, preferred_element_type=jnp...  20.8 us
    dot_general x4, matrix products, accumulate(): jnp.einsum('gxa,gay->xy', left_side, right_side, preferred_element_type=j...  20.3 us
    gather x8, local copies, waits for them, and re-layouts, factor(): resident = jnp.take(sink_slabs, sinks, axis=0)  17.1 us
    gather x8, local copies, waits for them, and re-layouts, factor(): gathered = jnp.take(received, slots, axis=1)  17.1 us
    all_to_all x1, waiting for transfers between devices, shards(): lax.all_to_all(outgoing, 'had', split_axis=1, concat_axis=1, tiled=True)  13.6 us
    all_to_all x1, starting transfers between devices, shards(): lax.all_to_all(outgoing, 'had', split_axis=1, concat_axis=1, tiled=True)  7.41 us
  transfers between devices with their start and end apart: 1, of which 1 were waited for; matrix products, arithmetic and copies ran while one was open for 0% of the time, Pallas kernels for 0%

commit v1 on v0

--- a/solution.py
+++ b/solution.py
@@ -61,7 +61,9 @@
     edge_local = (summed * edge_scale).astype(jnp.bfloat16)[None]
     left_ids = pair_list[:, 0]
     right_ids = pair_list[:, 1]
-    shard_rows = lax.all_gather(edge_local, "had", axis=0, tiled=True)
+    shard_rows = jnp.concatenate(
+        lax.all_to_all(jnp.stack([edge_local] * lax.axis_size("had")), "had", 0, 0), axis=0
+    )
     row_ids = jnp.arange(shard_rows.shape[0], dtype=jnp.int32)
     left_select = (left_ids[:, None] == row_ids[None, :]).astype(jnp.bfloat16)
     right_select = (right_ids[:, None] == row_ids[None, :]).astype(jnp.bfloat16)

time: 211 us -> 210 us (level)
  blocking collectives: 100 us -> 0 us
  starting transfers between devices: 7.41 us -> 92.1 us
  waiting for transfers between devices: 13.6 us -> 27.2 us
    all_gather x1 -> x0, blocking collectives: 100 us -> none  [shards(): shard_rows = lax.all_gather(edge_local, 'had', axis=0, tiled=True)]
    all_to_all x0 -> x1, starting transfers between devices: none -> 84.7 us  [shards(): lax.all_to_all(jnp.stack([edge_local] * lax.axis_size('had')), 'had', 0, 0)]
    all_to_all x0 -> x1, waiting for transfers between devices: none -> 13.6 us  [shards(): lax.all_to_all(jnp.stack([edge_local] * lax.axis_size('had')), 'had', 0, 0)]
  transfers between devices with their start and end apart: 1 -> 2, of which waited for: 1 -> 2; matrix products, arithmetic and copies ran while one was open for 0% -> 0% of each run, Pallas kernels for 0% -> 0%
where the time goes in v1:
time: 210 us
  starting transfers between devices  92.1 us (44%)
  matrix products  44.2 us (21%)
  local copies, waits for them, and re-layouts  38.8 us (18%)
  waiting for transfers between devices  27.2 us (13%)
  other arithmetic  5.67 us (3%)
    all_to_all x1, starting transfers between devices, shards(): lax.all_to_all(jnp.stack([edge_local] * lax.axis_size('had')), 'had', 0, 0)  84.7 us
    dot_general x4, matrix products, factor(): jnp.einsum('gxb,agb->gxa', resident, gathered, preferred_element_type=jnp...  20.8 us
    dot_general x4, matrix products, accumulate(): jnp.einsum('gxa,gay->xy', left_side, right_side, preferred_element_type=j...  20.4 us
    gather x8, local copies, waits for them, and re-layouts, factor(): resident = jnp.take(sink_slabs, sinks, axis=0)  17.1 us
    gather x8, local copies, waits for them, and re-layouts, factor(): gathered = jnp.take(received, slots, axis=1)  17.1 us
    all_to_all x1, waiting for transfers between devices, shards(): lax.all_to_all(jnp.stack([edge_local] * lax.axis_size('had')), 'had', 0, 0)  13.6 us
    all_to_all x1, waiting for transfers between devices, shards(): lax.all_to_all(outgoing, 'had', split_axis=1, concat_axis=1, tiled=True)  13.6 us
    all_to_all x1, starting transfers between devices, shards(): lax.all_to_all(outgoing, 'had', split_axis=1, concat_axis=1, tiled=True)  7.41 us
  transfers between devices with their start and end apart: 2, of which 2 were waited for; matrix products, arithmetic and copies ran while one was open for 0% of the time, Pallas kernels for 0%

profile of v1, /device:TPU:0, one launch (start us, length us, event | category | flops | bytes accessed | tf_op | source)
XLA Modules:
  0.0 209.7 jit_solution(10302668252594414979)
XLA Ops:
  0.6 0.0 copy-start
  0.7 0.7 fusion.45
  1.4 0.7 compare_and_fusion.4
  2.0 0.0 copy-done
  2.1 0.0 copy-start.1
  2.1 1.3 convolution_convert_fusion
  3.4 0.6 gather_fusion.4
  4.0 0.9 select_bitcast_fusion
  5.0 7.4 %all-to-all-start = ((bf16[128,16,128]{2,0,1:T(8,128)(2,1)}), bf16[128,16,128]{2,0,1:T(8,128)(2,1)S(1)}, u32[]{:S(2)}, u32[]{:S(2)}) async-start(bf16[128,16,128]{2,0,1:T(8,128)(2,1)} %select_bitcast_fusion), calls=%async_computation | async-start | bytes 1048576 | tf_op jit(solution)/shard_map/all_to_all | solution.py:33
  13.0 13.6 %all-to-all-done = bf16[128,16,128]{2,0,1:T(8,128)(2,1)S(1)} async-done(((bf16[128,16,128]{2,0,1:T(8,128)(2,1)}), bf16[128,16,128]{2,0,1:T(8,128)(2,1)S(1)}, u32[]{:S(2)}, u32[]{:S(2)}) %all-to-all-start) | async-done | bytes 524320 | tf_op jit(solution)/shard_map/all_to_all | solution.py:33
  26.7 0.0 copy-done.1
  26.7 0.0 copy-start.2
  26.7 81.4 %while.10 = (s32[]{:T(128)}, f32[128,128]{1,0:T(8,128)S(1)}, s32[]{:T(128)}, s32[512,2]{0,1:T(2,128)}, bf16[16,128,128]{2,1,0:T(8,128)(2,1)S(1)}, /*index=5*/s32...) while((s32[]{:T(128)}, f32[128,128]{1,0:T(8,128)S(1)}, ...), condition=%wide.region_1.4_spmd, body=%wide.region_0.3_spmd.sunk | while | flops 814765760 | bytes 29514672 | solution.py:60
  26.7 0.8 constant_dynamic-slice_fusion.3
  27.5 2.1 %gather_fusion = bf16[64,128,128]{2,1,0:T(8,128)(2,1)} fusion(bf16[128,16,128]{2,0,1:T(8,128)(2,1)S(1)} %get-tuple-element.188, s32[1024]{0:T(1024)S(1)} %pad_clamp_fusion.9), kind=kCustom, calls=%fused_computation.3.clone.clone.1 | custom fusion | bytes 4194560 | tf_op jit(solution)/shard_map/while/body/jit(_take)/gather | solution.py:41
  29.7 2.1 %gather_fusion.1 = bf16[64,128,128]{2,1,0:T(8,128)(2,1)} fusion(bf16[16,128,128]{2,1,0:T(8,128)(2,1)S(1)} %get-tuple-element.186, s32[1024]{0:T(1024)S(1)} %pad_clamp_fusion.10), kind=kCustom, calls=%fused_computation.2.clone.clone.1 | custom fusion | bytes 4194560 | tf_op jit(solution)/shard_map/while/body/jit(_take)/gather | solution.py:42
  31.8 5.2 %multiply_convert_fusion.4 = bf16[64,128,128]{2,1,0:T(8,128)(2,1)} fusion(bf16[64,128,128]{2,1,0:T(8,128)(2,1)} %gather_fusion, bf16[64,128,128]{2,1,0:T(8,128)(2,1)} %gather_fusion.1, pred[64]{0:T(512)(128)(4,1)S(1)} %get-tuple-element.152, pred[64]{0:T(512)(128)(4,1)S(1)} %get-tuple-element.153), kind=kOutput, calls=%fused_computation.5.clone.1 | convolution fusion | flops 272629760 | bytes 6291584 | tf_op jit(solution)/shard_map/while/body/gxb,agb->gxa/dot_general | solution.py:43
  37.0 2.1 %gather_fusion.2 = bf16[64,128,128]{2,1,0:T(8,128)(2,1)} fusion(bf16[128,16,128]{2,0,1:T(8,128)(2,1)S(1)} %get-tuple-element.188, s32[1024]{0:T(1024)S(1)} %pad_clamp_fusion.11), kind=kCustom, calls=%fused_computation.1.clone.clone.1 | custom fusion | bytes 4194560 | tf_op jit(solution)/shard_map/while/body/jit(_take)/gather | solution.py:41
  39.1 2.1 %gather_fusion.3 = bf16[64,128,128]{2,1,0:T(8,128)(2,1)} fusion(bf16[16,128,128]{2,1,0:T(8,128)(2,1)S(1)} %get-tuple-element.186, s32[1024]{0:T(1024)S(1)} %pad_clamp_fusion.12), kind=kCustom, calls=%fused_computation.clone.clone.1 | custom fusion | bytes 4194560 | tf_op jit(solution)/shard_map/while/body/jit(_take)/gather | solution.py:42
  41.3 0.6 compare_convert_fusion.2
  41.9 5.1 %fusion.64 = f32[128,128]{1,0:T(8,128)S(1)} fusion(f32[128,128]{1,0:T(8,128)S(1)} %get-tuple-element.171, bf16[64,128,128]{2,1,0:T(8,128)(2,1)} %multiply_convert_fusion.4, bf16[64,128,128]{2,1,0:T(8,128)(2,1)} %gather_fusion.2, bf16[64,128,128]{2,1,0:T(8,128)(2,1)} %gather_fusion.3, pred[64]{0:T(512)(128)(4,1)S(1)} %get-tuple-element.156, ...), kind=kOutput, calls=%fused_computation.20.clone.1 | convolution fusion | flops 542130176 | bytes 6422784 | tf_op jit(solution)/shard_map/while/body/gxa,gay->xy/dot_general | solution.py:55
  47.0 0.8 constant_dynamic-slice_fusion.3
  47.8 2.1 %gather_fusion = bf16[64,128,128]{2,1,0:T(8,128)(2,1)} fusion(bf16[128,16,128]{2,0,1:T(8,128)(2,1)S(1)} %get-tuple-element.188, s32[1024]{0:T(1024)S(1)} %pad_clamp_fusion.9), kind=kCustom, calls=%fused_computation.3.clone.clone.1 | custom fusion | bytes 4194560 | tf_op jit(solution)/shard_map/while/body/jit(_take)/gather | solution.py:41
  50.0 2.1 %gather_fusion.1 = bf16[64,128,128]{2,1,0:T(8,128)(2,1)} fusion(bf16[16,128,128]{2,1,0:T(8,128)(2,1)S(1)} %get-tuple-element.186, s32[1024]{0:T(1024)S(1)} %pad_clamp_fusion.10), kind=kCustom, calls=%fused_computation.2.clone.clone.1 | custom fusion | bytes 4194560 | tf_op jit(solution)/shard_map/while/body/jit(_take)/gather | solution.py:42
  52.1 5.2 %multiply_convert_fusion.4 = bf16[64,128,128]{2,1,0:T(8,128)(2,1)} fusion(bf16[64,128,128]{2,1,0:T(8,128)(2,1)} %gather_fusion, bf16[64,128,128]{2,1,0:T(8,128)(2,1)} %gather_fusion.1, pred[64]{0:T(512)(128)(4,1)S(1)} %get-tuple-element.152, pred[64]{0:T(512)(128)(4,1)S(1)} %get-tuple-element.153), kind=kOutput, calls=%fused_computation.5.clone.1 | convolution fusion | flops 272629760 | bytes 6291584 | tf_op jit(solution)/shard_map/while/body/gxb,agb->gxa/dot_general | solution.py:43
  57.4 2.1 %gather_fusion.2 = bf16[64,128,128]{2,1,0:T(8,128)(2,1)} fusion(bf16[128,16,128]{2,0,1:T(8,128)(2,1)S(1)} %get-tuple-element.188, s32[1024]{0:T(1024)S(1)} %pad_clamp_fusion.11), kind=kCustom, calls=%fused_computation.1.clone.clone.1 | custom fusion | bytes 4194560 | tf_op jit(solution)/shard_map/while/body/jit(_take)/gather | solution.py:41
  59.5 2.1 %gather_fusion.3 = bf16[64,128,128]{2,1,0:T(8,128)(2,1)} fusion(bf16[16,128,128]{2,1,0:T(8,128)(2,1)S(1)} %get-tuple-element.186, s32[1024]{0:T(1024)S(1)} %pad_clamp_fusion.12), kind=kCustom, calls=%fused_computation.clone.clone.1 | custom fusion | bytes 4194560 | tf_op jit(solution)/shard_map/while/body/jit(_take)/gather | solution.py:42
  61.6 0.6 compare_convert_fusion.2
  62.3 5.1 %fusion.64 = f32[128,128]{1,0:T(8,128)S(1)} fusion(f32[128,128]{1,0:T(8,128)S(1)} %get-tuple-element.171, bf16[64,128,128]{2,1,0:T(8,128)(2,1)} %multiply_convert_fusion.4, bf16[64,128,128]{2,1,0:T(8,128)(2,1)} %gather_fusion.2, bf16[64,128,128]{2,1,0:T(8,128)(2,1)} %gather_fusion.3, pred[64]{0:T(512)(128)(4,1)S(1)} %get-tuple-element.156, ...), kind=kOutput, calls=%fused_computation.20.clone.1 | convolution fusion | flops 542130176 | bytes 6422784 | tf_op jit(solution)/shard_map/while/body/gxa,gay->xy/dot_general | solution.py:55
  67.4 0.8 constant_dynamic-slice_fusion.3
  68.2 2.1 %gather_fusion = bf16[64,128,128]{2,1,0:T(8,128)(2,1)} fusion(bf16[128,16,128]{2,0,1:T(8,128)(2,1)S(1)} %get-tuple-element.188, s32[1024]{0:T(1024)S(1)} %pad_clamp_fusion.9), kind=kCustom, calls=%fused_computation.3.clone.clone.1 | custom fusion | bytes 4194560 | tf_op jit(solution)/shard_map/while/body/jit(_take)/gather | solution.py:41
  70.4 2.1 %gather_fusion.1 = bf16[64,128,128]{2,1,0:T(8,128)(2,1)} fusion(bf16[16,128,128]{2,1,0:T(8,128)(2,1)S(1)} %get-tuple-element.186, s32[1024]{0:T(1024)S(1)} %pad_clamp_fusion.10), kind=kCustom, calls=%fused_computation.2.clone.clone.1 | custom fusion | bytes 4194560 | tf_op jit(solution)/shard_map/while/body/jit(_take)/gather | solution.py:42
  72.5 5.2 %multiply_convert_fusion.4 = bf16[64,128,128]{2,1,0:T(8,128)(2,1)} fusion(bf16[64,128,128]{2,1,0:T(8,128)(2,1)} %gather_fusion, bf16[64,128,128]{2,1,0:T(8,128)(2,1)} %gather_fusion.1, pred[64]{0:T(512)(128)(4,1)S(1)} %get-tuple-element.152, pred[64]{0:T(512)(128)(4,1)S(1)} %get-tuple-element.153), kind=kOutput, calls=%fused_computation.5.clone.1 | convolution fusion | flops 272629760 | bytes 6291584 | tf_op jit(solution)/shard_map/while/body/gxb,agb->gxa/dot_general | solution.py:43
  77.7 2.1 %gather_fusion.2 = bf16[64,128,128]{2,1,0:T(8,128)(2,1)} fusion(bf16[128,16,128]{2,0,1:T(8,128)(2,1)S(1)} %get-tuple-element.188, s32[1024]{0:T(1024)S(1)} %pad_clamp_fusion.11), kind=kCustom, calls=%fused_computation.1.clone.clone.1 | custom fusion | bytes 4194560 | tf_op jit(solution)/shard_map/while/body/jit(_take)/gather | solution.py:41
  79.9 2.1 %gather_fusion.3 = bf16[64,128,128]{2,1,0:T(8,128)(2,1)} fusion(bf16[16,128,128]{2,1,0:T(8,128)(2,1)S(1)} %get-tuple-element.186, s32[1024]{0:T(1024)S(1)} %pad_clamp_fusion.12), kind=kCustom, calls=%fused_computation.clone.clone.1 | custom fusion | bytes 4194560 | tf_op jit(solution)/shard_map/while/body/jit(_take)/gather | solution.py:42
  82.0 0.6 compare_convert_fusion.2
  82.6 5.1 %fusion.64 = f32[128,128]{1,0:T(8,128)S(1)} fusion(f32[128,128]{1,0:T(8,128)S(1)} %get-tuple-element.171, bf16[64,128,128]{2,1,0:T(8,128)(2,1)} %multiply_convert_fusion.4, bf16[64,128,128]{2,1,0:T(8,128)(2,1)} %gather_fusion.2, bf16[64,128,128]{2,1,0:T(8,128)(2,1)} %gather_fusion.3, pred[64]{0:T(512)(128)(4,1)S(1)} %get-tuple-element.156, ...), kind=kOutput, calls=%fused_computation.20.clone.1 | convolution fusion | flops 542130176 | bytes 6422784 | tf_op jit(solution)/shard_map/while/body/gxa,gay->xy/dot_general | solution.py:55
  87.8 0.8 constant_dynamic-slice_fusion.3
  88.6 2.1 %gather_fusion = bf16[64,128,128]{2,1,0:T(8,128)(2,1)} fusion(bf16[128,16,128]{2,0,1:T(8,128)(2,1)S(1)} %get-tuple-element.188, s32[1024]{0:T(1024)S(1)} %pad_clamp_fusion.9), kind=kCustom, calls=%fused_computation.3.clone.clone.1 | custom fusion | bytes 4194560 | tf_op jit(solution)/shard_map/while/body/jit(_take)/gather | solution.py:41
  90.7 2.1 %gather_fusion.1 = bf16[64,128,128]{2,1,0:T(8,128)(2,1)} fusion(bf16[16,128,128]{2,1,0:T(8,128)(2,1)S(1)} %get-tuple-element.186, s32[1024]{0:T(1024)S(1)} %pad_clamp_fusion.10), kind=kCustom, calls=%fused_computation.2.clone.clone.1 | custom fusion | bytes 4194560 | tf_op jit(solution)/shard_map/while/body/jit(_take)/gather | solution.py:42
  92.9 5.2 %multiply_convert_fusion.4 = bf16[64,128,128]{2,1,0:T(8,128)(2,1)} fusion(bf16[64,128,128]{2,1,0:T(8,128)(2,1)} %gather_fusion, bf16[64,128,128]{2,1,0:T(8,128)(2,1)} %gather_fusion.1, pred[64]{0:T(512)(128)(4,1)S(1)} %get-tuple-element.152, pred[64]{0:T(512)(128)(4,1)S(1)} %get-tuple-element.153), kind=kOutput, calls=%fused_computation.5.clone.1 | convolution fusion | flops 272629760 | bytes 6291584 | tf_op jit(solution)/shard_map/while/body/gxb,agb->gxa/dot_general | solution.py:43
  98.1 2.1 %gather_fusion.2 = bf16[64,128,128]{2,1,0:T(8,128)(2,1)} fusion(bf16[128,16,128]{2,0,1:T(8,128)(2,1)S(1)} %get-tuple-element.188, s32[1024]{0:T(1024)S(1)} %pad_clamp_fusion.11), kind=kCustom, calls=%fused_computation.1.clone.clone.1 | custom fusion | bytes 4194560 | tf_op jit(solution)/shard_map/while/body/jit(_take)/gather | solution.py:41
  100.2 2.1 %gather_fusion.3 = bf16[64,128,128]{2,1,0:T(8,128)(2,1)} fusion(bf16[16,128,128]{2,1,0:T(8,128)(2,1)S(1)} %get-tuple-element.186, s32[1024]{0:T(1024)S(1)} %pad_clamp_fusion.12), kind=kCustom, calls=%fused_computation.clone.clone.1 | custom fusion | bytes 4194560 | tf_op jit(solution)/shard_map/while/body/jit(_take)/gather | solution.py:42
  102.3 0.6 compare_convert_fusion.2
  103.0 5.1 %fusion.64 = f32[128,128]{1,0:T(8,128)S(1)} fusion(f32[128,128]{1,0:T(8,128)S(1)} %get-tuple-element.171, bf16[64,128,128]{2,1,0:T(8,128)(2,1)} %multiply_convert_fusion.4, bf16[64,128,128]{2,1,0:T(8,128)(2,1)} %gather_fusion.2, bf16[64,128,128]{2,1,0:T(8,128)(2,1)} %gather_fusion.3, pred[64]{0:T(512)(128)(4,1)S(1)} %get-tuple-element.156, ...), kind=kOutput, calls=%fused_computation.20.clone.1 | convolution fusion | flops 542130176 | bytes 6422784 | tf_op jit(solution)/shard_map/while/body/gxa,gay->xy/dot_general | solution.py:55
  108.1 0.9 stack.3
  109.0 84.7 %all-to-all-start.1 = ((bf16[16,1,128,128]{3,2,1,0:T(8,128)(2,1)}), bf16[16,1,128,128]{3,2,1,0:T(8,128)(2,1)S(1)}, u32[]{:S(2)}, u32[]{:S(2)}) async-start(bf16[16,1,128,128]{3,2,1,0:T(8,128)(2,1)} %stack.3), calls=%async_computation.1 | async-start | bytes 1048576 | tf_op jit(solution)/shard_map/all_to_all | solution.py:65
  193.7 0.0 copy-done.2
  193.7 0.6 fusion.50
  194.3 13.6 %all-to-all-done.1 = bf16[16,1,128,128]{3,2,1,0:T(8,128)(2,1)S(1)} async-done(((bf16[16,1,128,128]{3,2,1,0:T(8,128)(2,1)}), bf16[16,1,128,128]{3,2,1,0:T(8,128)(2,1)S(1)}, u32[]{:S(2)}, u32[]{:S(2)}) %all-to-all-start.1) | async-done | bytes 524320 | tf_op jit(solution)/shard_map/all_to_all | solution.py:65
  207.9 0.4 fusion.35
  208.3 0.4 fusion.37
  208.8 0.9 fusion.34
  (28 shorter events, 0.2 us)
Async XLA Ops:
  0.6 1.4 copy-start
  2.1 24.6 %copy-start.1 = (bf16[16,128,128]{2,1,0:T(8,128)(2,1)S(1)}, bf16[16,128,128]{2,1,0:T(8,128)(2,1)}, u32[]{:S(2)}) copy-start(bf16[16,128,128]{2,1,0:T(8,128)(2,1)} %param.15) | copy-start | bytes 1572868
  5.0 21.7 %all-to-all-start = ((bf16[128,16,128]{2,0,1:T(8,128)(2,1)}), bf16[128,16,128]{2,0,1:T(8,128)(2,1)S(1)}, u32[]{:S(2)}, u32[]{:S(2)}) async-start(bf16[128,16,128]{2,0,1:T(8,128)(2,1)} %select_bitcast_fusion), calls=%async_computation | async-start | bytes 1048576 | tf_op jit(solution)/shard_map/all_to_all | solution.py:33
  26.7 167.0 %copy-start.2 = (s32[8,2]{0,1:T(2,128)S(1)}, s32[8,2]{0,1:T(2,128)}, u32[]{:S(2)}) copy-start(s32[8,2]{0,1:T(2,128)} %param.21) | copy-start | bytes 196
  109.0 98.9 %all-to-all-start.1 = ((bf16[16,1,128,128]{3,2,1,0:T(8,128)(2,1)}), bf16[16,1,128,128]{3,2,1,0:T(8,128)(2,1)S(1)}, u32[]{:S(2)}, u32[]{:S(2)}) async-start(bf16[16,1,128,128]{3,2,1,0:T(8,128)(2,1)} %stack.3), calls=%async_computation.1 | async-start | bytes 1048576 | tf_op jit(solution)/shard_map/all_to_all | solution.py:65
